TPU v7x, 32 devices: a whole 2x2x4 slice. The times are simulated.
32 devices in a mesh: ctx: 16 (over z, x, core), exp: 2 (over y).
Axes of the slice: x: 2, y: 2, z: 4, core: 2. Of those that a mesh axis runs over, the one named last changes fastest.
Arguments:
- resid: bfloat16 [2048, 2880], P(('ctx', 'exp')), may hold values from -3 to 3
- queries: bfloat16 [2048, 2048], P('ctx', 'exp'), may hold values from -8 to 8
- keys: bfloat16 [2048, 256], P('ctx'), may hold values from -8 to 8
- values: bfloat16 [2048, 256], P('ctx'), may hold values from -6 to 6
- sinks: float32 [32], P('exp'), may hold values from 0 to 6
- out_weight: bfloat16 [2048, 2880], P('exp'), may hold values from -0.125 to 0.125
- norm_gain: float32 [2880], replicated, may hold values from 0.5 to 1.5
- gate_weight: bfloat16 [16, 2880, 1536], P('ctx', None, 'exp'), may hold values from -0.109375 to 0.109375
- up_weight: bfloat16 [16, 2880, 1536], P('ctx', None, 'exp'), may hold values from -0.109375 to 0.109375
- down_weight: bfloat16 [16, 1536, 2880], P('ctx', 'exp'), may hold values from -0.15625 to 0.15625
- routes: int32 [2048, 4], P('ctx'), may hold values from 0 to 15, all different within a row; in each aligned block of 128 rows (0 to 127, 128 to 255, ...) at most 64 rows name the same one
- route_weights: float32 [2048, 4], P('ctx'), may hold values from 0.05 to 0.6
Outputs:
- block_out: bfloat16 [2048, 2880], P(('ctx', 'exp'))
Inputs may be any that keep to these rules, and one draw needn't show every extreme that they name: `routes`: in each aligned block of 128 rows no expert is named by more than 64 rows, a bound that some block reaches; a row names 4 different experts.
All inputs are finite; a program needn't handle non-finite values.
Results may differ from a plain program's by a relative error of at most 0.0085.
Values may be sent and summed in bfloat16 or wider, within the bound.
A program may use at most 128 MiB of HBM per device.

v0:
```python
import jax
import jax.numpy as jnp
from jax import lax
from jax.sharding import PartitionSpec as P

HD = 64
QH = 32
KVH = 4
TOP = 4
WIN = 128
NEG_FILL = -1e30
EPSILON = 1e-05


def shifted(array, axis, by):
    size = lax.axis_size(axis)
    pairs = [(i, i + by) for i in range(size) if 0 <= i + by < size]
    return lax.ppermute(array, axis, pairs)


def per_device(
    resid,
    queries,
    keys,
    values,
    sinks,
    out_weight,
    norm_gain,
    gate_weight,
    up_weight,
    down_weight,
    routes,
    route_weights,
):
    rows_here = queries.shape[0]
    local_heads = queries.shape[1] // HD
    per_group = QH // KVH
    kv_count = max(1, local_heads // per_group)
    head_reps = local_heads // kv_count
    exp_rank = lax.axis_index("exp")
    ctx_rank = lax.axis_index("ctx")
    kv_first = exp_rank * local_heads // per_group
    prior_keys, prior_values = shifted((keys, values), "ctx", 1)
    keys_ext = jnp.concatenate([prior_keys, keys], 0).reshape(rows_here + WIN, KVH, HD)
    values_ext = jnp.concatenate([prior_values, values], 0).reshape(rows_here + WIN, KVH, HD)
    keys_sel = lax.dynamic_slice_in_dim(keys_ext, kv_first, kv_count, 1)
    values_sel = lax.dynamic_slice_in_dim(values_ext, kv_first, kv_count, 1)
    query_four = queries.reshape(rows_here, kv_count, head_reps, HD)
    scores = jnp.einsum(
        "qgrd,kgd->grqk", query_four, keys_sel, preferred_element_type=jnp.float32
    ) * HD ** (-0.5)
    first_pos = ctx_rank * rows_here
    query_pos = first_pos + jnp.arange(rows_here, dtype=jnp.int32)
    key_pos = first_pos - WIN + jnp.arange(rows_here + WIN, dtype=jnp.int32)
    visible = (
        (key_pos[None, :] <= query_pos[:, None])
        & (key_pos[None, :] > query_pos[:, None] - WIN)
        & (key_pos[None, :] >= 0)
    )
    masked = jnp.where(visible[None, None], scores, NEG_FILL)
    sink_cols = sinks.reshape(kv_count, head_reps)[:, :, None]
    row_max = jnp.maximum(jnp.max(masked, axis=-1), sink_cols)
    exp_terms = jnp.where(visible[None, None], jnp.exp(masked - row_max[..., None]), 0.0)
    denominator = jnp.sum(exp_terms, axis=-1) + jnp.exp(sink_cols - row_max)
    soft_weights = (exp_terms / denominator[..., None]).astype(jnp.bfloat16)
    attended = jnp.einsum(
        "grqk,kgd->qgrd", soft_weights, values_sel, preferred_element_type=jnp.float32
    )
    attended = attended.reshape(rows_here, local_heads * HD).astype(jnp.bfloat16)
    projected = lax.psum_scatter(
        jnp.dot(attended, out_weight, preferred_element_type=jnp.float32),
        "exp",
        scatter_dimension=0,
        tiled=True,
    )
    after_attention = resid.astype(jnp.float32) + projected
    mean_square = jnp.mean(after_attention * after_attention, axis=-1, keepdims=True)
    normed = (after_attention * lax.rsqrt(mean_square + EPSILON) * norm_gain).astype(jnp.bfloat16)
    all_normed = lax.all_gather(normed, "exp", axis=0, tiled=True)
    n_experts = lax.axis_size("ctx")
    capacity = 2 * rows_here * TOP // n_experts
    width = all_normed.shape[1]
    flat_ids = routes.reshape(-1)
    one_hot = (flat_ids[:, None] == jnp.arange(n_experts, dtype=jnp.int32)[None, :]).astype(
        jnp.int32
    )
    rank_in = jnp.sum(jnp.cumsum(one_hot, axis=0) * one_hot, axis=1) - 1
    slot_index = flat_ids * capacity + rank_in
    token_of = jnp.arange(rows_here * TOP, dtype=jnp.int32) // TOP
    outgoing = (
        jnp.zeros((n_experts * capacity, width), jnp.bfloat16)
        .at[slot_index]
        .set(all_normed[token_of])
    )
    outgoing = outgoing.reshape(n_experts, capacity, width)
    gate_local = gate_weight[0]
    up_local = up_weight[0]
    down_local = down_weight[0]
    slot_block = lax.all_to_all(outgoing, "ctx", split_axis=0, concat_axis=0, tiled=True)
    block_shape = slot_block.shape
    flat_rows = slot_block.reshape(-1, block_shape[2])
    gate_val = jnp.dot(flat_rows, gate_local, preferred_element_type=jnp.float32)
    up_val = jnp.dot(flat_rows, up_local, preferred_element_type=jnp.float32)
    activated = (jax.nn.silu(gate_val) * up_val).astype(jnp.bfloat16)
    partial_rows = jnp.dot(activated, down_local, preferred_element_type=jnp.float32).astype(
        jnp.bfloat16
    )
    partial_out = partial_rows.reshape(block_shape)
    returned = lax.all_to_all(partial_out, "ctx", split_axis=0, concat_axis=0, tiled=True)
    flat_back = returned.reshape(n_experts * capacity, width)
    picked = flat_back[slot_index].reshape(rows_here, TOP, width)
    combined = jnp.sum(picked.astype(jnp.float32) * route_weights[:, :, None], axis=1)
    expert_mix = lax.psum_scatter(
        combined.astype(jnp.bfloat16), "exp", scatter_dimension=0, tiled=True
    ).astype(jnp.float32)
    return (after_attention + expert_mix).astype(jnp.bfloat16)


def solution(mesh):
    in_specs = (
        P(("ctx", "exp"), None),
        P("ctx", "exp"),
        P("ctx", None),
        P("ctx", None),
        P("exp"),
        P("exp", None),
        P(),
        P("ctx", None, "exp"),
        P("ctx", None, "exp"),
        P("ctx", "exp", None),
        P("ctx", None),
        P("ctx", None),
    )
    out_specs = P(("ctx", "exp"), None)
    return jax.shard_map(
        per_device, mesh=mesh, in_specs=in_specs, out_specs=out_specs, check_vma=False
    )
```

profile of v0, /device:TPU:0, one launch (start us, length us, event | category | flops | bytes accessed | tf_op | source)
XLA Modules:
  0.0 440.2 jit_solution(13573109594631216473)
XLA Ops:
  6.5 0.0 reduce-scatter.3.cloned.1.call-start
  6.5 2.5 collective-permute-start.1
  9.1 4.5 %collective-permute-start = (bf16[128,256]{1,0:T(8,128)(2,1)}, bf16[128,256]{1,0:T(8,128)(2,1)S(1)}, u32[]{:S(2)}, u32[]{:S(2)}) collective-permute-start(bf16[128,256]{1,0:T(8,128)(2,1)} %param.15), channel_id=1, source_target_pairs={{0,2},{2,4},{4,6},{6,8},{8,10},{10,12},{12,14},{14,16},{16,18},{18... | collective-permute-start | bytes 196616 | tf_op jit(solution)/shard_map/ppermute | solution.py:18
  13.6 0.1 and_and_fusion
  13.8 1.1 copy.21
  14.9 0.7 max.17
  15.6 0.0 collective-permute-done.1
  15.6 0.8 pad_maximum_fusion.1
  16.5 0.1 copy.20
  16.6 0.5 fusion.12
  17.1 0.1 broadcast_maximum_fusion
  17.2 0.5 fusion.14
  17.7 0.1 exponential_add_fusion
  17.8 0.0 collective-permute-done
  17.8 0.0 copy-done.3
  17.8 0.1 copy.19
  17.9 0.7 convolution_convert_fusion.1
  18.6 0.0 copy-start.2
  18.6 6.0 %fusion.29 = f32[128,2880]{1,0:T(8,128)} fusion(bf16[128,1024]{0,1:T(8,128)(2,1)S(1)} %bitcast.75, bf16[1024,2880]{0,1:T(8,128)(2,1)} %param.17), kind=kOutput, calls=%fused_computation.64 | convolution fusion | flops 754974720 | bytes 7634944 | tf_op jit(solution)/shard_map/dot_general | solution.py:71
  24.6 0.0 reduce-scatter.3.cloned.1.call-update
  24.6 0.1 copy.24
  24.8 0.1 eq.29
  24.9 0.1 eq.25
  25.0 1.2 reduce-window.6
  26.1 0.2 slice_reduce_fusion
  26.4 0.1 copy.23
  26.5 0.1 mul.75
  26.7 0.1 fusion.21
  26.8 23.8 %reduce-scatter.3.cloned.1.call-done = f32[64,2880]{1,0:T(8,128)} async-done(((f32[128,2880]{1,0:T(8,128)}), f32[64,2880]{1,0:T(8,128)}) %reduce-scatter.3.cloned.1.call-update) | async-done | bytes 737296 | tf_op jit(solution)/shard_map/reduce_scatter | solution.py:70
  50.5 1.3 multiply_reduce_fusion.1
  51.9 1.3 multiply_convert_fusion.1
  53.2 11.3 %all_gather.3 = bf16[128,2880]{1,0:T(8,128)(2,1)S(1)} all-gather(bf16[64,2880]{1,0:T(8,128)(2,1)S(1)} %multiply_convert_fusion.1), channel_id=1, replica_groups=mesh['ctx'=16,'exp'=2] {'exp'}, dimensions={0}, use_global_device_ids=true | all-gather | bytes 1105920 | tf_op jit(solution)/shard_map/all_gather | solution.py:79
  64.5 17.9 %scatter_custom_fusion = bf16[1024,2880]{1,0:T(8,128)(2,1)} fusion(s32[512]{0:T(512)S(1)} %bitcast.77, bf16[128,2880]{1,0:T(8,128)(2,1)S(1)} %all_gather.3, s32[1024]{0:T(1024)S(1)} %pad_clamp_fusion.1, bf16[]{:T(256)} %constant.72.clone.1), kind=kCustom, calls=%fused_computation.11 | custom fusion | bytes 5898242 | tf_op jit(solution)/shard_map/scatter | solution.py:93
  82.4 138.2 %all_to_all.10 = bf16[16,64,2880]{2,1,0:T(8,128)(2,1)S(1)} all-to-all(bf16[16,64,2880]{2,1,0:T(8,128)(2,1)} %bitcast.70), channel_id=1, replica_groups=mesh['ctx'=16,'exp'=2] {'ctx'}, dimensions={0} | all-to-all | bytes 11796480 | tf_op jit(solution)/shard_map/all_to_all | solution.py:99
  220.6 2.6 copy-done.1
  223.2 9.0 %fusion.1 = f32[1024,768]{1,0:T(8,128)} fusion(bf16[1024,2880]{1,0:T(8,128)(2,1)S(1)} %bitcast.71, bf16[1,2880,768]{2,1,0:T(8,128)(2,1)} %param.20), kind=kOutput, calls=%fused_computation.6 | convolution fusion | flops 4529848320 | bytes 13467648 | tf_op jit(solution)/shard_map/dot_general | solution.py:103
  232.2 16.5 %convolution_convert_fusion = bf16[1024,2880]{0,1:T(8,128)(2,1)} fusion(bf16[1,768,2880]{1,2,0:T(8,128)(2,1)} %param.21, f32[1024,768]{1,0:T(8,128)} %fusion.1, bf16[1024,2880]{1,0:T(8,128)(2,1)} %bitcast.72, bf16[1,2880,768]{2,1,0:T(8,128)(2,1)} %param.19), kind=kOutput, calls=%fused_computation.4 | convolution fusion | flops 9067364352 | bytes 23789568 | tf_op jit(solution)/shard_map/dot_general | solution.py:105
  248.8 8.5 %copy.27 = bf16[1024,2880]{1,0:T(8,128)(2,1)} copy(bf16[1024,2880]{0,1:T(8,128)(2,1)} %convolution_convert_fusion) | data formatting | bytes 11796480 | tf_op jit(solution)/shard_map/convert_element_type | solution.py:105
  257.3 4.8 %all-to-all-start.1 = ((bf16[16,64,2880]{2,1,0:T(8,128)(2,1)}), bf16[16,64,2880]{2,1,0:T(8,128)(2,1)}, u32[]{:S(2)}, u32[]{:S(2)}) async-start(bf16[16,64,2880]{2,1,0:T(8,128)(2,1)} %bitcast.69), calls=%async_computation.2 | async-start | bytes 12058624 | tf_op jit(solution)/shard_map/all_to_all | solution.py:109
  262.0 0.0 reduce-scatter.5.cloned.1.call-start
  262.1 0.1 copy.28
  262.2 109.3 %all-to-all-done.1 = bf16[16,64,2880]{2,1,0:T(8,128)(2,1)} async-done(((bf16[16,64,2880]{2,1,0:T(8,128)(2,1)}), bf16[16,64,2880]{2,1,0:T(8,128)(2,1)}, u32[]{:S(2)}, u32[]{:S(2)}) %all-to-all-start.1) | async-done | bytes 5898272 | tf_op jit(solution)/shard_map/all_to_all | solution.py:109
  371.5 9.5 %gather_fusion = bf16[512,2880]{1,0:T(8,128)(2,1)S(1)} fusion(bf16[1024,2880]{1,0:T(8,128)(2,1)} %bitcast.20, s32[1024]{0:T(1024)S(1)} %pad_clamp_fusion), kind=kCustom, calls=%fused_computation.1 | custom fusion | bytes 5900288 | tf_op jit(solution)/shard_map/gather | solution.py:111
  381.0 3.6 reshape.235
  384.6 8.0 %multiply_reduce_fusion = bf16[128,2880]{1,0:T(8,128)(2,1)} fusion(f32[128,4,2880]{2,1,0:T(4,128)} %reshape.235, f32[128,4]{1,0:T(8,128)S(1)} %copy.28), kind=kLoop, calls=%fused_computation.3 | loop fusion | flops 2580480 | bytes 6637568 | tf_op jit(solution)/shard_map/reduce_sum | solution.py:112
  392.6 0.0 reduce-scatter.5.cloned.1.call-update
  392.6 38.7 %reduce-scatter.5.cloned.1.call-done = bf16[64,2880]{1,0:T(8,128)(2,1)} async-done(((bf16[128,2880]{1,0:T(8,128)(2,1)}), bf16[64,2880]{1,0:T(8,128)(2,1)}) %reduce-scatter.5.cloned.1.call-update) | async-done | bytes 368656 | tf_op jit(solution)/shard_map/reduce_scatter | solution.py:113
  431.3 1.8 add_convert_fusion
  (25 shorter events, 0.1 us)
Async XLA Ops:
  6.5 11.2 %copy-start.3 = (bf16[128,256]{1,0:T(8,128)(2,1)S(1)}, bf16[128,256]{1,0:T(8,128)(2,1)}, u32[]{:S(2)}) copy-start(bf16[128,256]{1,0:T(8,128)(2,1)} %param.15) | copy-start | bytes 196612
  6.5 44.0 %reduce-scatter.3.cloned.1.call-start = ((), (), s32[]{:S(2)}) async-start(), calls=%async_computation.4 | async-start | bytes 2260992 | tf_op jit(solution)/shard_map/reduce_scatter | solution.py:70
  6.5 9.1 %collective-permute-start.1 = (bf16[128,256]{1,0:T(8,128)(2,1)}, bf16[128,256]{1,0:T(8,128)(2,1)S(1)}, u32[]{:S(2)}, u32[]{:S(2)}) collective-permute-start(bf16[128,256]{1,0:T(8,128)(2,1)} %param.14), channel_id=1, source_target_pairs={{0,2},{2,4},{4,6},{6,8},{8,10},{10,12},{12,14},{14,16},{16,18},{18... | collective-permute-start | bytes 196616 | tf_op jit(solution)/shard_map/ppermute | solution.py:18
  9.1 8.7 %collective-permute-start = (bf16[128,256]{1,0:T(8,128)(2,1)}, bf16[128,256]{1,0:T(8,128)(2,1)S(1)}, u32[]{:S(2)}, u32[]{:S(2)}) collective-permute-start(bf16[128,256]{1,0:T(8,128)(2,1)} %param.15), channel_id=1, source_target_pairs={{0,2},{2,4},{4,6},{6,8},{8,10},{10,12},{12,14},{14,16},{16,18},{18... | collective-permute-start | bytes 196616 | tf_op jit(solution)/shard_map/ppermute | solution.py:18
  18.6 6.0 %copy-start.5 = (s32[128,4]{0,1:T(4,128)S(1)}, s32[128,4]{0,1:T(4,128)}, u32[]{:S(2)}) copy-start(s32[128,4]{0,1:T(4,128)} %param.22) | copy-start | bytes 6148
  18.6 31.9 %copy-start.2 = (bf16[64,2880]{1,0:T(8,128)(2,1)S(1)}, bf16[64,2880]{1,0:T(8,128)(2,1)}, u32[]{:S(2)}) copy-start(bf16[64,2880]{1,0:T(8,128)(2,1)} %param.12) | copy-start | bytes 1105924
  24.6 27.3 %copy-start.4 = (f32[2880]{0:T(1024)S(1)}, f32[2880]{0:T(1024)}, u32[]{:S(2)}) copy-start(f32[2880]{0:T(1024)} %param.18) | copy-start | bytes 34564
  220.6 2.6 copy-start.1
  257.3 4.8 %copy-start.6 = (f32[128,4]{0,1:T(4,128)S(1)}, f32[128,4]{0,1:T(4,128)}, u32[]{:S(2)}) copy-start(f32[128,4]{0,1:T(4,128)} %param.23) | copy-start | bytes 6148
  257.3 114.2 %all-to-all-start.1 = ((bf16[16,64,2880]{2,1,0:T(8,128)(2,1)}), bf16[16,64,2880]{2,1,0:T(8,128)(2,1)}, u32[]{:S(2)}, u32[]{:S(2)}) async-start(bf16[16,64,2880]{2,1,0:T(8,128)(2,1)} %bitcast.69), calls=%async_computation.2 | async-start | bytes 12058624 | tf_op jit(solution)/shard_map/all_to_all | solution.py:109
  262.0 169.3 %reduce-scatter.5.cloned.1.call-start = ((), (), s32[]{:S(2)}) async-start(), calls=%async_computation.5 | async-start | bytes 1130496 | tf_op jit(solution)/shard_map/reduce_scatter | solution.py:113
  384.6 46.8 %copy-start = (f32[64,2880]{1,0:T(8,128)S(1)}, f32[64,2880]{1,0:T(8,128)}, u32[]{:S(2)}) copy-start(f32[64,2880]{1,0:T(8,128)} %reduce-scatter.3.cloned.1.call-done) | copy-start | bytes 2211844
Sparse Core Ops, SparseCore 0:
  24.8 25.7 reduce-scatter.2
  392.7 38.5 reduce-scatter.4
where the time goes:
time: 445 us; the launch traced here: 440 us
  waiting for transfers between devices  172 us (39%)
  blocking collectives  150 us (34%)
  local copies, waits for them, and re-layouts  45 us (10%)
  matrix products  32.8 us (7%)
  other arithmetic  15.4 us (3%)
  between operations  13.9 us (3%)
  starting transfers between devices  11.8 us (3%)
    all_to_all x1, blocking collectives, per_device(): lax.all_to_all(outgoing, 'ctx', split_axis=0, concat_axis=0, tiled=True)  138 us
    all_to_all x1, waiting for transfers between devices, per_device(): lax.all_to_all(partial_out, 'ctx', split_axis=0, concat_axis=0, tiled=True)  109 us
    reduce_scatter x1, waiting for transfers between devices, per_device(): lax.psum_scatter(combined.astype(jnp.bfloat16), 'exp', scatter_dimension=...  38.7 us
    reduce_scatter x1, waiting for transfers between devices, per_device(): lax.psum_scatter(jnp.dot(attended, out_weight, preferred_element_type=jnp...  23.8 us
    scatter x1, local copies, waits for them, and re-layouts, per_device(): outgoing = jnp.zeros((n_experts * capacity, width), jnp.bfloat16).at[slot...  17.9 us
    dot_general x1, matrix products, per_device(): jnp.dot(activated, down_local, preferred_element_type=jnp.float32)  16.5 us
    all_gather x1, blocking collectives, per_device(): all_normed = lax.all_gather(normed, 'exp', axis=0, tiled=True)  11.3 us
    gather x1, local copies, waits for them, and re-layouts, per_device(): picked = flat_back[slot_index].reshape(rows_here, TOP, width)  9.53 us
  transfers between devices with their start and end apart: 5, of which 3 were waited for; matrix products, arithmetic and copies ran while one was open for 1% of the time, Pallas kernels for 0%

commit v1 on v0

--- a/solution.py
+++ b/solution.py
@@ -10,6 +10,18 @@
 WIN = 128
 NEG_FILL = -1e30
 EPSILON = 1e-05
+
+
+def split_up(x, dim, devices):
+    dims = x.shape
+    blocks = x.reshape(*dims[:dim], devices, dims[dim] // devices, *dims[dim + 1 :])
+    return jnp.moveaxis(blocks, dim, 0)
+
+
+def in_order(pieces, dim):
+    lengths = list(pieces.shape[1:])
+    lengths[dim] *= pieces.shape[0]
+    return jnp.moveaxis(pieces, 0, dim).reshape(lengths)
 
 
 def shifted(array, axis, by):
@@ -96,7 +108,15 @@
     gate_local = gate_weight[0]
     up_local = up_weight[0]
     down_local = down_weight[0]
-    slot_block = lax.all_to_all(outgoing, "ctx", split_axis=0, concat_axis=0, tiled=True)
+    count, mine = (lax.axis_size("ctx"), lax.axis_index("ctx"))
+    pieces = split_up(outgoing, 0, count)
+    filled = pieces
+    for step in range(1, count):
+        target, source = ((mine + step) % count, (mine - step) % count)
+        sent = lax.dynamic_index_in_dim(pieces, target, 0)
+        other = lax.ppermute(sent, "ctx", [(i_2, (i_2 + step) % count) for i_2 in range(count)])
+        filled = lax.dynamic_update_slice_in_dim(filled, other, source, axis=0)
+    slot_block = in_order(filled, 0)
     block_shape = slot_block.shape
     flat_rows = slot_block.reshape(-1, block_shape[2])
     gate_val = jnp.dot(flat_rows, gate_local, preferred_element_type=jnp.float32)

time: 445 us -> 462 us (1.038)
  blocking collectives: 150 us -> 11.3 us
  starting transfers between devices: 11.8 us -> 82.1 us
  waiting for transfers between devices: 172 us -> 239 us
  local copies, waits for them, and re-layouts: 45 us -> 60.5 us
    all_to_all x1 -> x0, blocking collectives: 138 us -> none  [per_device(): lax.all_to_all(outgoing, 'ctx', split_axis=0, concat_axis=0, tiled=True)]
    ppermute x0 -> x15, starting transfers between devices: none -> 69 us  [per_device(): lax.ppermute(sent, 'ctx', [(i_2, (i_2 + step) % count) for i_2 in range(c...]
    ppermute x0 -> x15, waiting for transfers between devices: none -> 67.6 us  [per_device(): lax.ppermute(sent, 'ctx', [(i_2, (i_2 + step) % count) for i_2 in range(c...]
    dynamic_update_slice x0 -> x14, local copies, waits for them, and re-layouts: none -> 12.8 us  [per_device(): filled = lax.dynamic_update_slice_in_dim(filled, other, source, axis=0)]
    dynamic_slice x0 -> x2, local copies, waits for them, and re-layouts: none -> 5.25 us  [per_device(): sent = lax.dynamic_index_in_dim(pieces, target, 0)]
  transfers between devices with their start and end apart: 5 -> 20, of which waited for: 3 -> 9; matrix products, arithmetic and copies ran while one was open for 1% -> 4% of each run, Pallas kernels for 0% -> 0%
where the time goes in v1:
time: 462 us; the launch traced here: 457 us
  waiting for transfers between devices  239 us (52%)
  starting transfers between devices  82.1 us (18%)
  local copies, waits for them, and re-layouts  60.5 us (13%)
  matrix products  33.4 us (7%)
  other arithmetic  16.3 us (4%)
  between operations  14.4 us (3%)
  blocking collectives  11.3 us (2%)
    all_to_all x1, waiting for transfers between devices, per_device(): lax.all_to_all(partial_out, 'ctx', split_axis=0, concat_axis=0, tiled=True)  109 us
    ppermute x15, starting transfers between devices, per_device(): lax.ppermute(sent, 'ctx', [(i_2, (i_2 + step) % count) for i_2 in range(c...  69 us
    ppermute x15, waiting for transfers between devices, per_device(): lax.ppermute(sent, 'ctx', [(i_2, (i_2 + step) % count) for i_2 in range(c...  67.6 us
    reduce_scatter x1, waiting for transfers between devices, per_device(): lax.psum_scatter(combined.astype(jnp.bfloat16), 'exp', scatter_dimension=...  38.8 us
    reduce_scatter x1, waiting for transfers between devices, per_device(): lax.psum_scatter(jnp.dot(attended, out_weight, preferred_element_type=jnp...  23.7 us
    scatter x1, local copies, waits for them, and re-layouts, per_device(): outgoing = jnp.zeros((n_experts * capacity, width), jnp.bfloat16).at[slot...  17.9 us
    dot_general x1, matrix products, per_device(): jnp.dot(activated, down_local, preferred_element_type=jnp.float32)  16.5 us
    dynamic_update_slice x14, local copies, waits for them, and re-layouts, per_device(): filled = lax.dynamic_update_slice_in_dim(filled, other, source, axis=0)  12.8 us
  transfers between devices with their start and end apart: 20, of which 9 were waited for; matrix products, arithmetic and copies ran while one was open for 4% of the time, Pallas kernels for 0%

profile of v1, /device:TPU:0, one launch (start us, length us, event | category | flops | bytes accessed | tf_op | source)
XLA Modules:
  0.0 457.5 jit_solution(8786692037535295438)
XLA Ops:
  6.5 2.4 collective-permute-start.1
  8.9 4.5 collective-permute-start
  13.6 1.1 copy.21
  15.5 0.8 pad_maximum_fusion.1
  17.6 0.9 pad_maximum_fusion
  19.3 6.0 %fusion.29 = f32[128,2880]{1,0:T(8,128)} fusion(bf16[128,1024]{0,1:T(8,128)(2,1)S(1)} %bitcast.76, bf16[1024,2880]{0,1:T(8,128)(2,1)} %param.17), kind=kOutput, calls=%fused_computation.94 | convolution fusion | flops 754974720 | bytes 7634944 | tf_op jit(solution)/shard_map/dot_general | solution.py:83
  25.7 1.2 reduce-window.6
  27.5 23.7 %reduce-scatter.3.cloned.1.call-done = f32[64,2880]{1,0:T(8,128)} async-done(((f32[128,2880]{1,0:T(8,128)}), f32[64,2880]{1,0:T(8,128)}) %reduce-scatter.3.cloned.1.call-update) | async-done | bytes 737296 | tf_op jit(solution)/shard_map/reduce_scatter | solution.py:82
  51.2 1.3 multiply_reduce_fusion.1
  52.6 1.3 multiply_convert_fusion.2
  53.8 11.3 %all_gather.3 = bf16[128,2880]{1,0:T(8,128)(2,1)S(1)} all-gather(bf16[64,2880]{1,0:T(8,128)(2,1)S(1)} %multiply_convert_fusion.2), channel_id=1, replica_groups=mesh['ctx'=16,'exp'=2] {'exp'}, dimensions={0}, use_global_device_ids=true | all-gather | bytes 1105920 | tf_op jit(solution)/shard_map/all_gather | solution.py:91
  65.2 17.9 %scatter_custom_fusion = bf16[1024,2880]{1,0:T(8,128)(2,1)} fusion(s32[512]{0:T(512)S(1)} %bitcast.78, bf16[128,2880]{1,0:T(8,128)(2,1)S(1)} %all_gather.3, s32[1024]{0:T(1024)S(1)} %pad_clamp_fusion.1, bf16[]{:T(256)} %constant.257.clone.1), kind=kCustom, calls=%fused_computation.11 | custom fusion | bytes 5898242 | tf_op jit(solution)/shard_map/scatter | solution.py:105
  83.1 1.0 constant_dynamic-slice_fusion.14
  84.3 9.6 %collective-permute-done.2 = bf16[1,1,64,2880]{3,2,0,1:T(8,128)(2,1)} collective-permute-done((bf16[1,1,64,2880]{3,2,0,1:T(8,128)(2,1)S(1)}, bf16[1,1,64,2880]{3,2,0,1:T(8,128)(2,1)}, u32[]{:S(2)}, u32[]{:S(2)}) %collective-permute-start.2) | collective-permute-done | bytes 368672 | tf_op jit(solution)/shard_map/ppermute | solution.py:117
  94.0 4.2 constant_dynamic-slice_fusion
  98.6 2.2 collective-permute-start.6
  100.8 2.9 collective-permute-start.7
  103.8 9.2 %collective-permute-done.3 = bf16[1,1,64,2880]{3,2,0,1:T(8,128)(2,1)} collective-permute-done((bf16[1,1,64,2880]{3,2,0,1:T(8,128)(2,1)}, bf16[1,1,64,2880]{3,2,0,1:T(8,128)(2,1)}, u32[]{:S(2)}, u32[]{:S(2)}) %collective-permute-start.3) | collective-permute-done | bytes 368672 | tf_op jit(solution)/shard_map/ppermute | solution.py:117
  112.9 1.8 constant_dynamic-update-slice_fusion.13
  114.7 1.8 constant_dynamic-update-slice_fusion.12
  116.5 8.4 %collective-permute-start.10 = (bf16[1,1,64,2880]{3,2,0,1:T(8,128)(2,1)S(1)}, bf16[1,1,64,2880]{3,2,0,1:T(8,128)(2,1)S(1)}, u32[]{:S(2)}, u32[]{:S(2)}) collective-permute-start(bf16[1,1,64,2880]{3,2,0,1:T(8,128)(2,1)S(1)} %get-tuple-element.11), channel_id=1, source_target_pairs={{0,18},{2,20},{4,22},{6,24},{8,26},{10,28},{12,30},{14,0},{16,2},{... | collective-permute-start | bytes 1105928 | tf_op jit(solution)/shard_map/ppermute | solution.py:117
  124.8 0.8 constant_dynamic-update-slice_fusion.11
  125.6 42.1 %collective-permute-done.6 = bf16[1,1,64,2880]{3,2,0,1:T(8,128)(2,1)S(1)} collective-permute-done((bf16[1,1,64,2880]{3,2,0,1:T(8,128)(2,1)}, bf16[1,1,64,2880]{3,2,0,1:T(8,128)(2,1)S(1)}, u32[]{:S(2)}, u32[]{:S(2)}) %collective-permute-start.6) | collective-permute-done | bytes 368672 | tf_op jit(solution)/shard_map/ppermute | solution.py:117
  168.7 15.7 %collective-permute-start.12 = (bf16[1,1,64,2880]{3,2,0,1:T(8,128)(2,1)S(1)}, bf16[1,1,64,2880]{3,2,0,1:T(8,128)(2,1)S(1)}, u32[]{:S(2)}, u32[]{:S(2)}) collective-permute-start(bf16[1,1,64,2880]{3,2,0,1:T(8,128)(2,1)S(1)} %get-tuple-element.9), channel_id=1, source_target_pairs={{0,22},{2,24},{4,26},{6,28},{8,30},{10,0},{12,2},{14,4},{16,6},{18... | collective-permute-start | bytes 1105928 | tf_op jit(solution)/shard_map/ppermute | solution.py:117
  184.4 0.8 constant_dynamic-update-slice_fusion.9
  185.2 12.8 %collective-permute-start.13 = (bf16[1,1,64,2880]{3,2,0,1:T(8,128)(2,1)S(1)}, bf16[1,1,64,2880]{3,2,0,1:T(8,128)(2,1)S(1)}, u32[]{:S(2)}, u32[]{:S(2)}) collective-permute-start(bf16[1,1,64,2880]{3,2,0,1:T(8,128)(2,1)S(1)} %get-tuple-element.8), channel_id=1, source_target_pairs={{0,24},{2,26},{4,28},{6,30},{8,0},{10,2},{12,4},{14,6},{16,8},{18,... | collective-permute-start | bytes 1105928 | tf_op jit(solution)/shard_map/ppermute | solution.py:117
  198.0 0.8 constant_dynamic-update-slice_fusion.8
  198.8 14.8 %collective-permute-start.14 = (bf16[1,1,64,2880]{3,2,0,1:T(8,128)(2,1)S(1)}, bf16[1,1,64,2880]{3,2,0,1:T(8,128)(2,1)S(1)}, u32[]{:S(2)}, u32[]{:S(2)}) collective-permute-start(bf16[1,1,64,2880]{3,2,0,1:T(8,128)(2,1)S(1)} %get-tuple-element.7), channel_id=1, source_target_pairs={{0,26},{2,28},{4,30},{6,0},{8,2},{10,4},{12,6},{14,8},{16,10},{18,... | collective-permute-start | bytes 1105928 | tf_op jit(solution)/shard_map/ppermute | solution.py:117
  213.6 0.8 constant_dynamic-update-slice_fusion.7
  214.4 5.0 %collective-permute-start.15 = (bf16[1,1,64,2880]{3,2,0,1:T(8,128)(2,1)S(1)}, bf16[1,1,64,2880]{3,2,0,1:T(8,128)(2,1)S(1)}, u32[]{:S(2)}, u32[]{:S(2)}) collective-permute-start(bf16[1,1,64,2880]{3,2,0,1:T(8,128)(2,1)S(1)} %get-tuple-element.6), channel_id=1, source_target_pairs={{0,28},{2,30},{4,0},{6,2},{8,4},{10,6},{12,8},{14,10},{16,12},{18,... | collective-permute-start | bytes 1105928 | tf_op jit(solution)/shard_map/ppermute | solution.py:117
  219.3 0.8 constant_dynamic-update-slice_fusion.6
  220.1 7.0 %collective-permute-start.16 = (bf16[1,1,64,2880]{3,2,0,1:T(8,128)(2,1)S(1)}, bf16[1,1,64,2880]{3,2,0,1:T(8,128)(2,1)S(1)}, u32[]{:S(2)}, u32[]{:S(2)}) collective-permute-start(bf16[1,1,64,2880]{3,2,0,1:T(8,128)(2,1)S(1)} %get-tuple-element.5), channel_id=1, source_target_pairs={{0,30},{2,0},{4,2},{6,4},{8,6},{10,8},{12,10},{14,12},{16,14},{18,... | collective-permute-start | bytes 1105928 | tf_op jit(solution)/shard_map/ppermute | solution.py:117
  227.1 0.8 constant_dynamic-update-slice_fusion.5
  227.9 0.8 constant_dynamic-update-slice_fusion.4
  229.5 0.8 constant_dynamic-update-slice_fusion.2
  230.8 0.8 constant_dynamic-update-slice_fusion.1
  231.6 6.0 %collective-permute-done.16 = bf16[1,1,64,2880]{3,2,0,1:T(8,128)(2,1)S(1)} collective-permute-done((bf16[1,1,64,2880]{3,2,0,1:T(8,128)(2,1)S(1)}, bf16[1,1,64,2880]{3,2,0,1:T(8,128)(2,1)S(1)}, u32[]{:S(2)}, u32[]{:S(2)}) %collective-permute-start.16) | collective-permute-done | bytes 368672 | tf_op jit(solution)/shard_map/ppermute | solution.py:117
  237.5 0.8 constant_dynamic-update-slice_fusion
  238.3 9.7 %fusion.1 = f32[1024,768]{1,0:T(8,128)} fusion(bf16[1024,2880]{1,0:T(8,128)(2,1)} %bitcast.72, bf16[1,2880,768]{2,1,0:T(8,128)(2,1)} %param.20), kind=kOutput, calls=%fused_computation.6 | convolution fusion | flops 4529848320 | bytes 13467648 | tf_op jit(solution)/shard_map/dot_general | solution.py:123
  248.0 16.5 %convolution_convert_fusion = bf16[1024,2880]{0,1:T(8,128)(2,1)} fusion(bf16[1,768,2880]{1,2,0:T(8,128)(2,1)} %param.21, f32[1024,768]{1,0:T(8,128)} %fusion.1, bf16[1024,2880]{1,0:T(8,128)(2,1)} %bitcast.73, bf16[1,2880,768]{2,1,0:T(8,128)(2,1)} %param.19), kind=kOutput, calls=%fused_computation.4 | convolution fusion | flops 9067364352 | bytes 23789568 | tf_op jit(solution)/shard_map/dot_general | solution.py:125
  264.5 8.5 %copy.27 = bf16[1024,2880]{1,0:T(8,128)(2,1)} copy(bf16[1024,2880]{0,1:T(8,128)(2,1)} %convolution_convert_fusion) | data formatting | bytes 11796480 | tf_op jit(solution)/shard_map/convert_element_type | solution.py:125
  273.0 6.1 %all-to-all-start = ((bf16[16,64,2880]{2,1,0:T(8,128)(2,1)}), bf16[16,64,2880]{2,1,0:T(8,128)(2,1)}, u32[]{:S(2)}, u32[]{:S(2)}) async-start(bf16[16,64,2880]{2,1,0:T(8,128)(2,1)} %bitcast.69), calls=%async_computation.1 | async-start | bytes 12058624 | tf_op jit(solution)/shard_map/all_to_all | solution.py:129
  279.4 109.3 %all-to-all-done = bf16[16,64,2880]{2,1,0:T(8,128)(2,1)} async-done(((bf16[16,64,2880]{2,1,0:T(8,128)(2,1)}), bf16[16,64,2880]{2,1,0:T(8,128)(2,1)}, u32[]{:S(2)}, u32[]{:S(2)}) %all-to-all-start) | async-done | bytes 5898272 | tf_op jit(solution)/shard_map/all_to_all | solution.py:129
  388.7 9.5 %gather_fusion = bf16[512,2880]{1,0:T(8,128)(2,1)S(1)} fusion(bf16[1024,2880]{1,0:T(8,128)(2,1)} %bitcast.20, s32[1024]{0:T(1024)S(1)} %pad_clamp_fusion), kind=kCustom, calls=%fused_computation.1 | custom fusion | bytes 5900288 | tf_op jit(solution)/shard_map/gather | solution.py:131
  398.2 3.6 reshape.227
  401.8 8.0 %multiply_reduce_fusion = bf16[128,2880]{1,0:T(8,128)(2,1)} fusion(f32[128,4,2880]{2,1,0:T(4,128)} %reshape.227, f32[128,4]{1,0:T(8,128)S(1)} %copy.28), kind=kLoop, calls=%fused_computation.3 | loop fusion | flops 2580480 | bytes 6637568 | tf_op jit(solution)/shard_map/reduce_sum | solution.py:132
  409.8 38.8 %reduce-scatter.5.cloned.1.call-done = bf16[64,2880]{1,0:T(8,128)(2,1)} async-done(((bf16[128,2880]{1,0:T(8,128)(2,1)}), bf16[64,2880]{1,0:T(8,128)(2,1)}) %reduce-scatter.5.cloned.1.call-update) | async-done | bytes 368656 | tf_op jit(solution)/shard_map/reduce_scatter | solution.py:133
  448.6 1.8 add_convert_fusion
  (66 shorter events, 6.6 us)
Async XLA Ops:
  6.5 44.7 %reduce-scatter.3.cloned.1.call-start = ((), (), s32[]{:S(2)}) async-start(), calls=%async_computation.3 | async-start | bytes 2260992 | tf_op jit(solution)/shard_map/reduce_scatter | solution.py:82
  6.5 9.0 %collective-permute-start.1 = (bf16[128,256]{1,0:T(8,128)(2,1)}, bf16[128,256]{1,0:T(8,128)(2,1)S(1)}, u32[]{:S(2)}, u32[]{:S(2)}) collective-permute-start(bf16[128,256]{1,0:T(8,128)(2,1)} %param.14), channel_id=1, source_target_pairs={{0,2},{2,4},{4,6},{6,8},{8,10},{10,12},{12,14},{14,16},{16,18},{18... | collective-permute-start | bytes 196616 | tf_op jit(solution)/shard_map/ppermute | solution.py:30
  8.9 8.7 %collective-permute-start = (bf16[128,256]{1,0:T(8,128)(2,1)}, bf16[128,256]{1,0:T(8,128)(2,1)S(1)}, u32[]{:S(2)}, u32[]{:S(2)}) collective-permute-start(bf16[128,256]{1,0:T(8,128)(2,1)} %param.15), channel_id=1, source_target_pairs={{0,2},{2,4},{4,6},{6,8},{8,10},{10,12},{12,14},{14,16},{16,18},{18... | collective-permute-start | bytes 196616 | tf_op jit(solution)/shard_map/ppermute | solution.py:30
  19.3 6.0 %copy-start.3 = (s32[128,4]{0,1:T(4,128)S(1)}, s32[128,4]{0,1:T(4,128)}, u32[]{:S(2)}) copy-start(s32[128,4]{0,1:T(4,128)} %param.22) | copy-start | bytes 6148
  19.3 31.9 %copy-start.1 = (bf16[64,2880]{1,0:T(8,128)(2,1)S(1)}, bf16[64,2880]{1,0:T(8,128)(2,1)}, u32[]{:S(2)}) copy-start(bf16[64,2880]{1,0:T(8,128)(2,1)} %param.12) | copy-start | bytes 1105924
  19.3 33.2 %copy-start.2 = (f32[2880]{0:T(1024)S(1)}, f32[2880]{0:T(1024)}, u32[]{:S(2)}) copy-start(f32[2880]{0:T(1024)} %param.18) | copy-start | bytes 34564
  84.1 9.9 %collective-permute-start.2 = (bf16[1,1,64,2880]{3,2,0,1:T(8,128)(2,1)S(1)}, bf16[1,1,64,2880]{3,2,0,1:T(8,128)(2,1)}, u32[]{:S(2)}, u32[]{:S(2)}) collective-permute-start(bf16[1,1,64,2880]{3,2,0,1:T(8,128)(2,1)S(1)} %constant_dynamic-slice_fusion.14), channel_id=1, source_target_pairs={{0,2},{2,4},{4,6},{6,8},{8,10},{10,12},{12,14},{14,16},{16,18},{18... | collective-permute-start | bytes 1105928 | tf_op jit(solution)/shard_map/ppermute | solution.py:117
  98.2 14.7 %collective-permute-start.3 = (bf16[1,1,64,2880]{3,2,0,1:T(8,128)(2,1)}, bf16[1,1,64,2880]{3,2,0,1:T(8,128)(2,1)}, u32[]{:S(2)}, u32[]{:S(2)}) collective-permute-start(bf16[1,1,64,2880]{3,2,0,1:T(8,128)(2,1)} %get-tuple-element.18), channel_id=1, source_target_pairs={{0,4},{2,6},{4,8},{6,10},{8,12},{10,14},{12,16},{14,18},{16,20},{1... | collective-permute-start | bytes 1105928 | tf_op jit(solution)/shard_map/ppermute | solution.py:117
  98.2 16.5 %collective-permute-start.4 = (bf16[1,1,64,2880]{3,2,0,1:T(8,128)(2,1)}, bf16[1,1,64,2880]{3,2,0,1:T(8,128)(2,1)}, u32[]{:S(2)}, u32[]{:S(2)}) collective-permute-start(bf16[1,1,64,2880]{3,2,0,1:T(8,128)(2,1)} %get-tuple-element.17), channel_id=1, source_target_pairs={{0,6},{2,8},{4,10},{6,12},{8,14},{10,16},{12,18},{14,20},{16,22},{... | collective-permute-start | bytes 1105928 | tf_op jit(solution)/shard_map/ppermute | solution.py:117
  98.5 17.9 %collective-permute-start.5 = (bf16[1,1,64,2880]{3,2,0,1:T(8,128)(2,1)}, bf16[1,1,64,2880]{3,2,0,1:T(8,128)(2,1)S(1)}, u32[]{:S(2)}, u32[]{:S(2)}) collective-permute-start(bf16[1,1,64,2880]{3,2,0,1:T(8,128)(2,1)} %get-tuple-element.16), channel_id=1, source_target_pairs={{0,8},{2,10},{4,12},{6,14},{8,16},{10,18},{12,20},{14,22},{16,24},... | collective-permute-start | bytes 1105928 | tf_op jit(solution)/shard_map/ppermute | solution.py:117
  98.6 69.1 %collective-permute-start.6 = (bf16[1,1,64,2880]{3,2,0,1:T(8,128)(2,1)}, bf16[1,1,64,2880]{3,2,0,1:T(8,128)(2,1)S(1)}, u32[]{:S(2)}, u32[]{:S(2)}) collective-permute-start(bf16[1,1,64,2880]{3,2,0,1:T(8,128)(2,1)} %get-tuple-element.15), channel_id=1, source_target_pairs={{0,10},{2,12},{4,14},{6,16},{8,18},{10,20},{12,22},{14,24},{16,26}... | collective-permute-start | bytes 1105928 | tf_op jit(solution)/shard_map/ppermute | solution.py:117
  100.8 67.8 %collective-permute-start.7 = (bf16[1,1,64,2880]{3,2,0,1:T(8,128)(2,1)}, bf16[1,1,64,2880]{3,2,0,1:T(8,128)(2,1)S(1)}, u32[]{:S(2)}, u32[]{:S(2)}) collective-permute-start(bf16[1,1,64,2880]{3,2,0,1:T(8,128)(2,1)} %get-tuple-element.14), channel_id=1, source_target_pairs={{0,12},{2,14},{4,16},{6,18},{8,20},{10,22},{12,24},{14,26},{16,28}... | collective-permute-start | bytes 1105928 | tf_op jit(solution)/shard_map/ppermute | solution.py:117
  112.9 72.3 %collective-permute-start.8 = (bf16[1,1,64,2880]{3,2,0,1:T(8,128)(2,1)}, bf16[1,1,64,2880]{3,2,0,1:T(8,128)(2,1)S(1)}, u32[]{:S(2)}, u32[]{:S(2)}) collective-permute-start(bf16[1,1,64,2880]{3,2,0,1:T(8,128)(2,1)} %get-tuple-element.13), channel_id=1, source_target_pairs={{0,14},{2,16},{4,18},{6,20},{8,22},{10,24},{12,26},{14,28},{16,30}... | collective-permute-start | bytes 1105928 | tf_op jit(solution)/shard_map/ppermute | solution.py:117
  114.7 84.0 %collective-permute-start.9 = (bf16[1,1,64,2880]{3,2,0,1:T(8,128)(2,1)S(1)}, bf16[1,1,64,2880]{3,2,0,1:T(8,128)(2,1)S(1)}, u32[]{:S(2)}, u32[]{:S(2)}) collective-permute-start(bf16[1,1,64,2880]{3,2,0,1:T(8,128)(2,1)S(1)} %get-tuple-element.12), channel_id=1, source_target_pairs={{0,16},{2,18},{4,20},{6,22},{8,24},{10,26},{12,28},{14,30},{16,0},... | collective-permute-start | bytes 1105928 | tf_op jit(solution)/shard_map/ppermute | solution.py:117
  116.5 97.9 %collective-permute-start.10 = (bf16[1,1,64,2880]{3,2,0,1:T(8,128)(2,1)S(1)}, bf16[1,1,64,2880]{3,2,0,1:T(8,128)(2,1)S(1)}, u32[]{:S(2)}, u32[]{:S(2)}) collective-permute-start(bf16[1,1,64,2880]{3,2,0,1:T(8,128)(2,1)S(1)} %get-tuple-element.11), channel_id=1, source_target_pairs={{0,18},{2,20},{4,22},{6,24},{8,26},{10,28},{12,30},{14,0},{16,2},{... | collective-permute-start | bytes 1105928 | tf_op jit(solution)/shard_map/ppermute | solution.py:117
  167.7 52.4 %collective-permute-start.11 = (bf16[1,1,64,2880]{3,2,0,1:T(8,128)(2,1)S(1)}, bf16[1,1,64,2880]{3,2,0,1:T(8,128)(2,1)S(1)}, u32[]{:S(2)}, u32[]{:S(2)}) collective-permute-start(bf16[1,1,64,2880]{3,2,0,1:T(8,128)(2,1)S(1)} %get-tuple-element.10), channel_id=1, source_target_pairs={{0,20},{2,22},{4,24},{6,26},{8,28},{10,30},{12,0},{14,2},{16,4},{1... | collective-permute-start | bytes 1105928 | tf_op jit(solution)/shard_map/ppermute | solution.py:117
  168.7 59.2 %collective-permute-start.12 = (bf16[1,1,64,2880]{3,2,0,1:T(8,128)(2,1)S(1)}, bf16[1,1,64,2880]{3,2,0,1:T(8,128)(2,1)S(1)}, u32[]{:S(2)}, u32[]{:S(2)}) collective-permute-start(bf16[1,1,64,2880]{3,2,0,1:T(8,128)(2,1)S(1)} %get-tuple-element.9), channel_id=1, source_target_pairs={{0,22},{2,24},{4,26},{6,28},{8,30},{10,0},{12,2},{14,4},{16,6},{18... | collective-permute-start | bytes 1105928 | tf_op jit(solution)/shard_map/ppermute | solution.py:117
  185.2 43.5 %collective-permute-start.13 = (bf16[1,1,64,2880]{3,2,0,1:T(8,128)(2,1)S(1)}, bf16[1,1,64,2880]{3,2,0,1:T(8,128)(2,1)S(1)}, u32[]{:S(2)}, u32[]{:S(2)}) collective-permute-start(bf16[1,1,64,2880]{3,2,0,1:T(8,128)(2,1)S(1)} %get-tuple-element.8), channel_id=1, source_target_pairs={{0,24},{2,26},{4,28},{6,30},{8,0},{10,2},{12,4},{14,6},{16,8},{18,... | collective-permute-start | bytes 1105928 | tf_op jit(solution)/shard_map/ppermute | solution.py:117
  198.8 30.7 %collective-permute-start.14 = (bf16[1,1,64,2880]{3,2,0,1:T(8,128)(2,1)S(1)}, bf16[1,1,64,2880]{3,2,0,1:T(8,128)(2,1)S(1)}, u32[]{:S(2)}, u32[]{:S(2)}) collective-permute-start(bf16[1,1,64,2880]{3,2,0,1:T(8,128)(2,1)S(1)} %get-tuple-element.7), channel_id=1, source_target_pairs={{0,26},{2,28},{4,30},{6,0},{8,2},{10,4},{12,6},{14,8},{16,10},{18,... | collective-permute-start | bytes 1105928 | tf_op jit(solution)/shard_map/ppermute | solution.py:117
  214.4 16.4 %collective-permute-start.15 = (bf16[1,1,64,2880]{3,2,0,1:T(8,128)(2,1)S(1)}, bf16[1,1,64,2880]{3,2,0,1:T(8,128)(2,1)S(1)}, u32[]{:S(2)}, u32[]{:S(2)}) collective-permute-start(bf16[1,1,64,2880]{3,2,0,1:T(8,128)(2,1)S(1)} %get-tuple-element.6), channel_id=1, source_target_pairs={{0,28},{2,30},{4,0},{6,2},{8,4},{10,6},{12,8},{14,10},{16,12},{18,... | collective-permute-start | bytes 1105928 | tf_op jit(solution)/shard_map/ppermute | solution.py:117
  220.1 17.4 %collective-permute-start.16 = (bf16[1,1,64,2880]{3,2,0,1:T(8,128)(2,1)S(1)}, bf16[1,1,64,2880]{3,2,0,1:T(8,128)(2,1)S(1)}, u32[]{:S(2)}, u32[]{:S(2)}) collective-permute-start(bf16[1,1,64,2880]{3,2,0,1:T(8,128)(2,1)S(1)} %get-tuple-element.5), channel_id=1, source_target_pairs={{0,30},{2,0},{4,2},{6,4},{8,6},{10,8},{12,10},{14,12},{16,14},{18,... | collective-permute-start | bytes 1105928 | tf_op jit(solution)/shard_map/ppermute | solution.py:117
  273.0 6.2 %copy-start.4 = (f32[128,4]{0,1:T(4,128)S(1)}, f32[128,4]{0,1:T(4,128)}, u32[]{:S(2)}) copy-start(f32[128,4]{0,1:T(4,128)} %param.23) | copy-start | bytes 6148
  273.0 115.7 %all-to-all-start = ((bf16[16,64,2880]{2,1,0:T(8,128)(2,1)}), bf16[16,64,2880]{2,1,0:T(8,128)(2,1)}, u32[]{:S(2)}, u32[]{:S(2)}) async-start(bf16[16,64,2880]{2,1,0:T(8,128)(2,1)} %bitcast.69), calls=%async_computation.1 | async-start | bytes 12058624 | tf_op jit(solution)/shard_map/all_to_all | solution.py:129
  279.2 169.4 %reduce-scatter.5.cloned.1.call-start = ((), (), s32[]{:S(2)}) async-start(), calls=%async_computation.4 | async-start | bytes 1130496 | tf_op jit(solution)/shard_map/reduce_scatter | solution.py:133
  401.8 46.8 %copy-start = (f32[64,2880]{1,0:T(8,128)S(1)}, f32[64,2880]{1,0:T(8,128)}, u32[]{:S(2)}) copy-start(f32[64,2880]{1,0:T(8,128)} %reduce-scatter.3.cloned.1.call-done) | copy-start | bytes 2211844
Sparse Core Ops, SparseCore 0:
  25.4 25.7 reduce-scatter.2
  409.9 38.5 reduce-scatter.4
